TPU v7x, 256 devices: a whole 4x4x8 slice. The times are simulated.
256 devices in a mesh: blk: 16 (over z, y_lo), img: 16 (over x, y_hi, core).
Axes of the slice: x: 4, y: 4 (y_hi: 2, y_lo: 2; y = y_hi * 2 + y_lo), z: 8, core: 2. Of those that a mesh axis runs over, the one named last changes fastest.
Arguments:
- hidden: bfloat16 [16, 2048, 1536], P('img', 'blk'), may hold values from -6 to 6
- text_hidden: bfloat16 [16, 154, 1536], P('img'), may hold values from -6 to 6
- latent: float32 [16, 64, 2048], P('img', 'blk'), may hold values from -6 to 6
- image_mod: float32 [16, 6, 1536], P('img'), may hold values from -10 to 10
- text_mod: float32 [16, 2, 1536], P('img'), may hold values from -3 to 3
- final_mod: float32 [16, 2, 1536], P('img'), may hold values from -3 to 3
- counts: int32 [16], P('img'), may hold values from 512 to 2048, as said below
- step_index: int32 [16], P('img'), may hold values from 0 to 7
- qkv_weight: bfloat16 [1536, 2304], P(None, 'img'), may hold values from -0.21875 to 0.21875
- text_weight: bfloat16 [1536, 1536], replicated, may hold values from -0.21875 to 0.21875
- out_weight: bfloat16 [768, 1536], replicated, may hold values from -0.21875 to 0.21875
- mlp_in_weight: bfloat16 [1536, 3072], P(None, 'img'), may hold values from -0.15625 to 0.15625
- mlp_out_weight: bfloat16 [3072, 1536], P(None, 'img'), may hold values from -0.109375 to 0.109375
- final_weight: bfloat16 [1536, 64], replicated, may hold values from -0.15625 to 0.15625
- conv_weight: bfloat16 [144, 512], replicated, may hold values from -0.5 to 0.5
- conv_bias: float32 [512], replicated, may hold values from -3 to 3
Outputs:
- velocity: float32 [16, 64, 2048], P('img', 'blk')
- next_latent: float32 [16, 64, 2048], P('img', 'blk')
- features: bfloat16 [16, 64, 128, 512], P('img', 'blk')
Inputs may be any that keep to these rules, and one draw needn't show every extreme that they name: `counts`: each count is a multiple of 128; in every draw one image has all 2048 patches.
All inputs are finite; a program needn't handle non-finite values.
Results may differ from a plain program's by a relative error of at most 0.015.
The roundings to bfloat16 on the way count: a program that leaves them out, or rounds other values in their place, can miss the bound.
Values may be sent and summed in bfloat16 or wider, within the bound.
No kernel may reach another device: no remote copies, remote signals or barrier semaphores. Data moves between devices by JAX's collectives and lax.ppermute only.
A program may use at most 128 MiB of HBM per device.

v0:
```python
import jax
import jax.numpy as jnp
from jax import lax
from jax.sharding import PartitionSpec as P

HEAD = 64
CH = 16
HEADS = 12
W_P = 64
STEPS = 8
norm_eps = 1e-06
sigma_shift = 3.0
vae_scale = 1.5305
vae_offset = 0.0609
masked_score = -1e30


def padded(x, sides, width):
    for axis, dim in sides:
        size, length = (lax.axis_size(axis), x.shape[dim])
        up = [(i, (i + 1) % size) for i in range(size - 1)]
        down = [(j, i) for i, j in up]
        last = lax.slice_in_dim(x, length - width, length, axis=dim)
        first = lax.slice_in_dim(x, 0, width, axis=dim)
        before = lax.ppermute(last, axis, up)
        after = lax.ppermute(first, axis, down)
        x = jnp.concatenate([before, x, after], axis=dim)
    return x


def modulate(inputs, shift_row, scale_row):
    values = inputs.astype(jnp.float32)
    center = jnp.mean(values, axis=-1, keepdims=True)
    spread = jnp.mean(jnp.square(values - center), axis=-1, keepdims=True)
    normed = (values - center) * lax.rsqrt(spread + norm_eps)
    return (normed * (1.0 + scale_row) + shift_row).astype(jnp.bfloat16)


def plan(step_value):
    remain = 1.0 - step_value / STEPS
    return sigma_shift * remain / (1.0 + (sigma_shift - 1.0) * remain)


def absorb(running, queries, key_rows, value_rows, key_valid):
    run_max, run_sum, run_out = running
    key_heads = key_rows.reshape(key_rows.shape[0], HEADS, HEAD)
    value_heads = value_rows.reshape(value_rows.shape[0], HEADS, HEAD)
    scores = (
        jnp.einsum("qhd,khd->hqk", queries, key_heads, preferred_element_type=jnp.float32) * 0.125
    )
    scores = jnp.where(key_valid[None, None, :], scores, masked_score)
    new_max = jnp.maximum(run_max, jnp.max(scores, axis=-1))
    factor = jnp.exp(run_max - new_max)
    numer = jnp.exp(scores - new_max[:, :, None])
    run_sum = run_sum * factor + jnp.sum(numer, axis=-1)
    run_out = run_out * factor[:, :, None] + jnp.einsum(
        "hqk,khd->hqd", numer.astype(jnp.bfloat16), value_heads, preferred_element_type=jnp.float32
    )
    return (new_max, run_sum, run_out)


def per_device(
    hidden,
    text_hidden,
    latent,
    image_mod,
    text_mod,
    final_mod,
    counts,
    step_index,
    qkv_weight,
    text_weight,
    out_weight,
    mlp_in_weight,
    mlp_out_weight,
    final_weight,
    conv_weight,
    conv_bias,
):
    tok_rows = hidden.shape[1]
    width_attn = HEADS * HEAD
    patch_count = counts[0]
    image_terms = image_mod[0]
    image_in = modulate(hidden[0], image_terms[0], image_terms[1])
    text_in = modulate(text_hidden[0], text_mod[0, 0], text_mod[0, 1])
    text_kv = jnp.dot(text_in, text_weight, preferred_element_type=jnp.float32).astype(jnp.bfloat16)
    qkv_all = jnp.dot(
        image_in,
        lax.all_gather(qkv_weight, "img", axis=1, tiled=True),
        preferred_element_type=jnp.float32,
    ).astype(jnp.bfloat16)
    queries = qkv_all[:, :width_attn].reshape(tok_rows, HEADS, HEAD)
    own_keys = qkv_all[:, width_attn : 2 * width_attn]
    own_values = qkv_all[:, 2 * width_attn :]
    start_state = (
        jnp.full((HEADS, tok_rows), -jnp.inf, jnp.float32),
        jnp.zeros((HEADS, tok_rows), jnp.float32),
        jnp.zeros((HEADS, tok_rows, HEAD), jnp.float32),
    )
    text_valid = jnp.ones((text_kv.shape[0],), dtype=bool)
    text_state = absorb(
        start_state, queries, text_kv[:, :width_attn], text_kv[:, width_attn:], text_valid
    )
    folded = text_state
    key_rows = lax.all_gather(own_keys, "blk", axis=0, tiled=True)
    value_rows = lax.all_gather(own_values, "blk", axis=0, tiled=True)
    blocks = key_rows.shape[0] // tok_rows
    key_blocks = key_rows.reshape(blocks, tok_rows, width_attn)
    value_blocks = value_rows.reshape(blocks, tok_rows, width_attn)

    def visit(running, block_item):
        key_block, value_block, block_pos = block_item
        block_first = block_pos * tok_rows
        key_valid = block_first + jnp.arange(tok_rows, dtype=jnp.int32) < patch_count
        running = absorb(running, queries, key_block, value_block, key_valid)
        return (running, None)

    folded, _ = lax.scan(
        visit, folded, (key_blocks, value_blocks, jnp.arange(blocks, dtype=jnp.int32))
    )
    run_max, run_sum, run_out = folded
    attended = (
        (run_out / run_sum[:, :, None])
        .transpose(1, 0, 2)
        .reshape(tok_rows, width_attn)
        .astype(jnp.bfloat16)
    )
    projected = jnp.dot(attended, out_weight, preferred_element_type=jnp.float32)
    updated = hidden[0].astype(jnp.float32) + image_terms[2] * projected
    mlp_in = modulate(updated, image_terms[3], image_terms[4])
    mlp_hidden = jax.nn.gelu(
        jnp.dot(
            mlp_in,
            lax.all_gather(mlp_in_weight, "img", axis=1, tiled=True),
            preferred_element_type=jnp.float32,
        ),
        approximate=True,
    ).astype(jnp.bfloat16)
    mlp_out = jnp.dot(
        mlp_hidden,
        lax.all_gather(mlp_out_weight, "img", axis=1, tiled=True),
        preferred_element_type=jnp.float32,
    )
    refined = updated + image_terms[5] * mlp_out
    final_in = modulate(refined, final_mod[0, 0], final_mod[0, 1])
    predicted = jnp.dot(final_in, final_weight, preferred_element_type=jnp.float32)
    patch_rows = tok_rows // W_P
    lat_rows = 2 * patch_rows
    vel_lat = (
        predicted.reshape(patch_rows, W_P, 2, 2, CH)
        .transpose(0, 2, 1, 3, 4)
        .reshape(lat_rows, 2 * W_P * CH)
    )
    global_rows = lax.axis_index("blk") * lat_rows + jnp.arange(lat_rows, dtype=jnp.int32)
    live_rows = (global_rows < 2 * (patch_count // W_P))[:, None]
    velocity = jnp.where(live_rows, vel_lat, 0.0)
    step_value = step_index[0].astype(jnp.float32)
    sigma_gap = plan(step_value + 1.0) - plan(step_value)
    next_lat = jnp.where(live_rows, latent[0] + sigma_gap * vel_lat, 0.0)
    scaled = jnp.where(live_rows, next_lat / vae_scale + vae_offset, 0.0).astype(jnp.bfloat16)
    framed = padded(scaled, (("blk", 0),), 1)
    padded_grid = jnp.pad(framed.reshape(lat_rows + 2, 2 * W_P, CH), ((0, 0), (1, 1), (0, 0)))
    columns = jnp.concatenate(
        [
            padded_grid[row_off : row_off + lat_rows, col_off : col_off + 2 * W_P, :]
            for row_off in range(3)
            for col_off in range(3)
        ],
        axis=-1,
    ).reshape(lat_rows * 2 * W_P, 9 * CH)
    feature = jnp.dot(columns, conv_weight, preferred_element_type=jnp.float32) + conv_bias
    feature = jnp.where(live_rows[:, :, None], feature.reshape(lat_rows, 2 * W_P, -1), 0.0).astype(
        jnp.bfloat16
    )
    return (velocity[None], next_lat[None], feature[None])


def solution(mesh):
    placed = (
        P("img", "blk", None),
        P("img", None, None),
        P("img", "blk", None),
        P("img", None, None),
        P("img", None, None),
        P("img", None, None),
        P("img"),
        P("img"),
        P(None, "img"),
        P(),
        P(),
        P(None, "img"),
        P(None, "img"),
        P(),
        P(),
        P(),
    )
    return jax.shard_map(
        per_device,
        mesh=mesh,
        in_specs=placed,
        out_specs=(P("img", "blk", None), P("img", "blk", None), P("img", "blk", None, None)),
        check_vma=False,
    )
```

profile of v0, /device:TPU:104, one launch (start us, length us, event | category | flops | bytes accessed | tf_op | source)
XLA Modules:
  0.0 461.3 jit_solution(7038986041568204380)
XLA Ops:
  9.3 1.4 slice_reduce_fusion.2
  13.1 71.2 %all-gather.6.cloned.1.call-done = bf16[1536,2304]{0,1:T(8,128)(2,1)} async-done(((bf16[1536,144]{0,1:T(8,128)(2,1)}), bf16[1536,2304]{0,1:T(8,128)(2,1)}) %all-gather.6.cloned.1.call-update) | async-done | bytes 7077904 | tf_op jit(solution)/shard_map/all_gather | solution.py:89
  84.3 5.6 %convolution_convert_fusion = bf16[128,2304]{1,0:T(8,128)(2,1)S(1)} fusion(bf16[1536,2304]{0,1:T(8,128)(2,1)} %all-gather.6.cloned.1.call-done, bf16[1,128,1536]{2,1,0:T(8,128)(2,1)} %param.18, f32[1536]{0:T(1024)S(1)} %get-tuple-element.72, f32[1536]{0:T(1024)S(1)} %get-tuple-element.76, f32[128]{0:T(128)S(1)} %add_rsqrt_fusion.3, ...), kind=kOutput, calls=%fused_computation.13 | convolution fusion | flops 907444224 | bytes 8074240 | tf_op jit(solution)/shard_map/dot_general | solution.py:87
  93.8 3.3 convolution_convert_fusion.1
  100.4 1.8 copy.32
  105.3 64.7 %all-gather.8.cloned.1.call-done = bf16[2048,768]{1,0:T(8,128)(2,1)} async-done(((bf16[128,768]{1,0:T(8,128)(2,1)}), bf16[2048,768]{1,0:T(8,128)(2,1)}) %all-gather.8.cloned.1.call-update) | async-done | bytes 3145744 | tf_op jit(solution)/shard_map/all_gather | solution.py:105
  170.0 81.6 %all-gather.10.cloned.1.call-done = bf16[2048,768]{1,0:T(8,128)(2,1)} async-done(((bf16[128,768]{1,0:T(8,128)(2,1)}), bf16[2048,768]{1,0:T(8,128)(2,1)}) %all-gather.10.cloned.1.call-update) | async-done | bytes 3145744 | tf_op jit(solution)/shard_map/all_gather | solution.py:106
  252.1 138.2 %while.14 = (s32[]{:T(128)}, f32[12,128]{1,0:T(8,128)S(1)}, f32[12,128]{1,0:T(8,128)}, f32[12,128,64]{1,2,0:T(8,128)}, s32[16]{0:T(128)}, /*index=5*/s32[]{:T(12...) while((s32[]{:T(128)}, f32[12,128]{1,0:T(8,128)S(1)}, ...), condition=%wide.region_9.10_spmd, body=%wide.region_6.9_spmd.sunk | while | flops 51907840 | bytes 5407121 | solution.py:118
  258.7 2.0 convolution_add_fusion.4
  267.3 2.0 convolution_add_fusion.4
  276.0 2.0 convolution_add_fusion.4
  284.6 2.0 convolution_add_fusion.4
  293.2 2.0 convolution_add_fusion.4
  301.9 2.0 convolution_add_fusion.4
  310.5 2.0 convolution_add_fusion.4
  319.2 2.0 convolution_add_fusion.4
  327.8 2.0 convolution_add_fusion.4
  336.5 2.0 convolution_add_fusion.4
  345.1 2.0 convolution_add_fusion.4
  353.7 2.0 convolution_add_fusion.4
  362.3 2.0 convolution_add_fusion.4
  371.0 2.0 convolution_add_fusion.4
  379.7 2.0 convolution_add_fusion.4
  388.3 2.0 convolution_add_fusion.4
  391.4 1.6 fusion.76
  393.3 25.1 %all-gather.14.cloned.1.call-done = bf16[3072,1536]{0,1:T(8,128)(2,1)} async-done(((bf16[3072,96]{0,1:T(8,128)(2,1)}), bf16[3072,1536]{0,1:T(8,128)(2,1)}) %all-gather.14.cloned.1.call-update) | async-done | bytes 9437200 | tf_op jit(solution)/shard_map/all_gather | solution.py:141
  418.4 13.7 %fusion.77 = (f32[128]{0:T(128)S(1)}, f32[128,1536]{1,0:T(8,128)}) fusion(f32[128,1536]{1,0:T(8,128)S(1)} %get-tuple-element.127, bf16[3072,1536]{0,1:T(8,128)(2,1)} %all-gather.14.cloned.1.call-done, bf16[1536,3072]{0,1:T(8,128)(2,1)} %all-gather.12.cloned.1.call-done, f32[1536]{0:T(1024)S(1)} %copy-done.9, f32[1536]{0:T(1024)S(1)} %copy-done.7, ...), kind=kOutput, calls=%fused_computation.130 | convolution fusion | flops 2421030912 | bytes 20467200 | tf_op jit(solution)/shard_map/dot_general | solution.py:139
  433.6 1.5 fusion.58
  435.9 5.6 %collective-permute-start = (bf16[1,2048]{1,0:T(2,128)(2,1)S(1)}, bf16[1,2048]{1,0:T(2,128)(2,1)S(1)}, u32[]{:S(2)}, u32[]{:S(2)}) collective-permute-start(bf16[1,2048]{1,0:T(2,128)(2,1)S(1)} %get-tuple-element.120), channel_id=1, source_target_pairs={{0,16},{16,32},{32,48},{48,64},{64,80},{80,96},{96,112},{112,128},... | collective-permute-start | bytes 12296 | tf_op jit(solution)/shard_map/ppermute | solution.py:25
  441.5 1.9 collective-permute-start.1
  445.2 3.9 collective-permute-done.1
  450.5 2.0 concatenate.40
  (253 shorter events, 118.0 us)
Async XLA Ops:
  7.2 384.2 %copy-start = (bf16[768,1536]{1,0:T(8,128)(2,1)S(1)}, bf16[768,1536]{1,0:T(8,128)(2,1)}, u32[]{:S(2)}) copy-start(bf16[768,1536]{1,0:T(8,128)(2,1)} %param.28) | copy-start | bytes 7077892
  7.2 77.1 %all-gather.6.cloned.1.call-start = ((), (), s32[]{:S(2)}) async-start(), calls=%async_computation | async-start | bytes 7520256 | tf_op jit(solution)/shard_map/all_gather | solution.py:89
  7.9 162.1 %all-gather.8.cloned.1.call-start = ((), (), s32[]{:S(2)}) async-start(), calls=%async_computation.1 | async-start | bytes 3342336 | tf_op jit(solution)/shard_map/all_gather | solution.py:105
  84.3 9.0 %copy-start.5 = (f32[1,2,1536]{2,1,0:T(2,128)S(1)}, f32[1,2,1536]{2,1,0:T(2,128)}, u32[]{:S(2)}) copy-start(f32[1,2,1536]{2,1,0:T(2,128)} %param.22) | copy-start | bytes 36868
  89.9 3.5 copy-start.1
  90.7 160.9 %all-gather.10.cloned.1.call-start = ((), (), s32[]{:S(2)}) async-start(), calls=%async_computation.2 | async-start | bytes 3342336 | tf_op jit(solution)/shard_map/all_gather | solution.py:106
  91.5 301.8 %all-gather.12.cloned.1.call-start = ((), (), s32[]{:S(2)}) async-start(), calls=%async_computation.3 | async-start | bytes 10027008 | tf_op jit(solution)/shard_map/all_gather | solution.py:134
  92.1 326.3 %all-gather.14.cloned.1.call-start = ((), (), s32[]{:S(2)}) async-start(), calls=%async_computation.4 | async-start | bytes 10027008 | tf_op jit(solution)/shard_map/all_gather | solution.py:141
  93.8 3.8 copy-start.6
  93.8 5.6 %copy-start.3 = (f32[1,4,2048]{2,1,0:T(4,128)S(1)}, f32[1,4,2048]{2,1,0:T(4,128)}, u32[]{:S(2)}) copy-start(f32[1,4,2048]{2,1,0:T(4,128)} %param.20) | copy-start | bytes 98308
  98.9 153.2 %copy-start.12 = (pred[4]{0:T(512)(128)(4,1)}, pred[4]{0:T(512)(128)(4,1)S(1)}, u32[]{:S(2)}) copy-start(pred[4]{0:T(512)(128)(4,1)S(1)} %add_compare_fusion.1) | copy-start | bytes 16
  390.3 28.1 %copy-start.7 = (f32[1536]{0:T(1024)S(1)}, f32[1536]{0:T(1024)}, u32[]{:S(2)}) copy-start(f32[1536]{0:T(1024)} %get-tuple-element.75) | copy-start | bytes 18436
  390.3 28.1 %copy-start.8 = (f32[1536]{0:T(1024)S(1)}, f32[1536]{0:T(1024)}, u32[]{:S(2)}) copy-start(f32[1536]{0:T(1024)} %get-tuple-element.71) | copy-start | bytes 18436
  390.3 28.1 %copy-start.9 = (f32[1536]{0:T(1024)S(1)}, f32[1536]{0:T(1024)}, u32[]{:S(2)}) copy-start(f32[1536]{0:T(1024)} %get-tuple-element.74) | copy-start | bytes 18436
  418.4 15.2 %copy-start.10 = (f32[1536]{0:T(1024)S(1)}, f32[1536]{0:T(1024)}, u32[]{:S(2)}) copy-start(f32[1536]{0:T(1024)} %get-tuple-element.77) | copy-start | bytes 18436
  418.4 15.2 %copy-start.11 = (f32[1536]{0:T(1024)S(1)}, f32[1536]{0:T(1024)}, u32[]{:S(2)}) copy-start(f32[1536]{0:T(1024)} %get-tuple-element.78) | copy-start | bytes 18436
  418.4 15.2 %copy-start.15 = (bf16[1536,64]{0,1:T(8,128)(2,1)S(1)}, bf16[1536,64]{0,1:T(8,128)(2,1)}, u32[]{:S(2)}) copy-start(bf16[1536,64]{0,1:T(8,128)(2,1)} %param.31) | copy-start | bytes 589828
  418.4 17.4 %copy-start.4 = (f32[1,4,2048]{2,1,0:T(4,128)S(1)}, f32[1,4,2048]{2,1,0:T(4,128)}, u32[]{:S(2)}) copy-start(f32[1,4,2048]{2,1,0:T(4,128)} %param.20) | copy-start | bytes 98308
  418.4 17.4 %copy-start.13 = (pred[4]{0:T(512)(128)(4,1)S(1)}, pred[4]{0:T(512)(128)(4,1)}, u32[]{:S(2)}) copy-start(pred[4]{0:T(512)(128)(4,1)} %copy-done.12) | copy-start | bytes 16
  432.1 12.3 %copy-start.2 = (f32[512,16]{1,0:T(8,128)S(1)}, f32[512,16]{1,0:T(8,128)}, u32[]{:S(2)}) copy-start(f32[512,16]{1,0:T(8,128)} %squeeze.13) | copy-start | bytes 98308
  432.1 12.3 %copy-start.14 = (pred[512]{0:T(512)(128)(4,1)S(1)}, pred[512]{0:T(512)(128)(4,1)}, u32[]{:S(2)}) copy-start(pred[512]{0:T(512)(128)(4,1)} %broadcast_bitcast_fusion) | copy-start | bytes 1540
  433.6 18.9 %copy-start.16 = (f32[512]{0:T(512)S(1)}, f32[512]{0:T(512)}, u32[]{:S(2)}) copy-start(f32[512]{0:T(512)} %param.33) | copy-start | bytes 6148
  435.9 9.3 %collective-permute-start = (bf16[1,2048]{1,0:T(2,128)(2,1)S(1)}, bf16[1,2048]{1,0:T(2,128)(2,1)S(1)}, u32[]{:S(2)}, u32[]{:S(2)}) collective-permute-start(bf16[1,2048]{1,0:T(2,128)(2,1)S(1)} %get-tuple-element.120), channel_id=1, source_target_pairs={{0,16},{16,32},{32,48},{48,64},{64,80},{80,96},{96,112},{112,128},... | collective-permute-start | bytes 12296 | tf_op jit(solution)/shard_map/ppermute | solution.py:25
  441.5 7.7 %collective-permute-start.1 = (bf16[1,2048]{1,0:T(2,128)(2,1)S(1)}, bf16[1,2048]{1,0:T(2,128)(2,1)S(1)}, u32[]{:S(2)}, u32[]{:S(2)}) collective-permute-start(bf16[1,2048]{1,0:T(2,128)(2,1)S(1)} %get-tuple-element.121), channel_id=1, source_target_pairs={{16,0},{32,16},{48,32},{64,48},{80,64},{96,80},{112,96},{128,112},... | collective-permute-start | bytes 12296 | tf_op jit(solution)/shard_map/ppermute | solution.py:26
Sparse Core Ops, SparseCore 0:
  10.7 73.5 all-gather.5
  90.9 79.1 all-gather.7
  171.8 79.7 all-gather.9
  254.2 81.4 all-gather.11
  338.2 80.0 all-gather.13
where the time goes:
time: 464 us; the launch traced here: 461 us
  waiting for transfers between devices  249 us (54%)
  matrix products  81.7 us (18%)
  local copies, waits for them, and re-layouts  52.2 us (11%)
  other arithmetic  44.4 us (10%)
  between operations  15.6 us (3%)
  loops' own time  10.9 us (2%)
  starting transfers between devices  7.67 us (2%)
    all_gather x1, waiting for transfers between devices, per_device(): value_rows = lax.all_gather(own_values, 'blk', axis=0, tiled=True)  81.6 us
    all_gather x1, waiting for transfers between devices, per_device(): lax.all_gather(qkv_weight, 'img', axis=1, tiled=True)  71.2 us
    all_gather x1, waiting for transfers between devices, per_device(): key_rows = lax.all_gather(own_keys, 'blk', axis=0, tiled=True)  64.7 us
    dynamic_slice x64, local copies, waits for them, and re-layouts, per_device(): lax.scan(visit, folded, (key_blocks, value_blocks, jnp.arange(blocks, dty...  41.5 us
    dot_general x17, matrix products, absorb(): jnp.einsum('hqk,khd->hqd', numer.astype(jnp.bfloat16), value_heads, prefe...  33.1 us
    all_gather x1, waiting for transfers between devices, per_device(): lax.all_gather(mlp_out_weight, 'img', axis=1, tiled=True)  25.1 us
    dot_general x17, matrix products, absorb(): jnp.einsum('qhd,khd->hqk', queries, key_heads, preferred_element_type=jnp...  21.6 us
    add x16, other arithmetic, absorb(): run_sum = run_sum * factor + jnp.sum(numer, axis=-1)  20.8 us
  transfers between devices with their start and end apart: 7, of which 5 were waited for; matrix products, arithmetic and copies ran while one was open for 32% of the time, Pallas kernels for 0%

commit v1 on v0

--- a/solution.py
+++ b/solution.py
@@ -13,6 +13,11 @@
 vae_scale = 1.5305
 vae_offset = 0.0609
 masked_score = -1e30
+
+
+def gather_over(x, axis, d):
+    stack = jnp.stack([x] * lax.axis_size(axis))
+    return jnp.concatenate(lax.all_to_all(stack, axis, 0, 0), axis=d)
 
 
 def padded(x, sides, width):
@@ -137,9 +142,7 @@
         approximate=True,
     ).astype(jnp.bfloat16)
     mlp_out = jnp.dot(
-        mlp_hidden,
-        lax.all_gather(mlp_out_weight, "img", axis=1, tiled=True),
-        preferred_element_type=jnp.float32,
+        mlp_hidden, gather_over(mlp_out_weight, "img", 1), preferred_element_type=jnp.float32
     )
     refined = updated + image_terms[5] * mlp_out
     final_in = modulate(refined, final_mod[0, 0], final_mod[0, 1])

time: 464 us -> 537 us (1.16)
  waiting for transfers between devices: 249 us -> 313 us
  local copies, waits for them, and re-layouts: 52.2 us -> 57.6 us
    all_gather x1, waiting for transfers between devices: 64.7 us -> 155 us  [per_device(): key_rows = lax.all_gather(own_keys, 'blk', axis=0, tiled=True)]
    all_gather x1 -> x0, waiting for transfers between devices: 25.1 us -> none  [per_device(): lax.all_gather(mlp_out_weight, 'img', axis=1, tiled=True)]
  transfers between devices with their start and end apart: 7 -> 7, of which waited for: 5 -> 4; matrix products, arithmetic and copies ran while one was open for 32% -> 29% of each run, Pallas kernels for 0% -> 0%
where the time goes in v1:
time: 537 us; the launch traced here: 534 us
  waiting for transfers between devices  313 us (58%)
  matrix products  81.5 us (15%)
  local copies, waits for them, and re-layouts  57.6 us (11%)
  other arithmetic  44.5 us (8%)
  between operations  15.6 us (3%)
  starting transfers between devices  11.1 us (2%)
  loops' own time  10.7 us (2%)
    all_gather x1, waiting for transfers between devices, per_device(): key_rows = lax.all_gather(own_keys, 'blk', axis=0, tiled=True)  155 us
    all_gather x1, waiting for transfers between devices, per_device(): value_rows = lax.all_gather(own_values, 'blk', axis=0, tiled=True)  82 us
    all_gather x1, waiting for transfers between devices, per_device(): lax.all_gather(qkv_weight, 'img', axis=1, tiled=True)  71.2 us
    dynamic_slice x64, local copies, waits for them, and re-layouts, per_device(): lax.scan(visit, folded, (key_blocks, value_blocks, jnp.arange(blocks, dty...  42 us
    dot_general x17, matrix products, absorb(): jnp.einsum('hqk,khd->hqd', numer.astype(jnp.bfloat16), value_heads, prefe...  33 us
    dot_general x17, matrix products, absorb(): jnp.einsum('qhd,khd->hqk', queries, key_heads, preferred_element_type=jnp...  21.5 us
    add x16, other arithmetic, absorb(): run_sum = run_sum * factor + jnp.sum(numer, axis=-1)  20.9 us
    dot_general x1, matrix products, per_device(): jnp.dot(mlp_hidden, gather_over(mlp_out_weight, 'img', 1), preferred_elem...  13.7 us
  transfers between devices with their start and end apart: 7, of which 4 were waited for; matrix products, arithmetic and copies ran while one was open for 29% of the time, Pallas kernels for 0%

profile of v1, /device:TPU:104, one launch (start us, length us, event | category | flops | bytes accessed | tf_op | source)
XLA Modules:
  0.0 534.3 jit_solution(10384403005119726184)
XLA Ops:
  13.1 71.2 %all-gather.5.cloned.1.call-done = bf16[1536,2304]{0,1:T(8,128)(2,1)} async-done(((bf16[1536,144]{0,1:T(8,128)(2,1)}), bf16[1536,2304]{0,1:T(8,128)(2,1)}) %all-gather.5.cloned.1.call-update) | async-done | bytes 7077904 | tf_op jit(solution)/shard_map/all_gather | solution.py:94
  84.3 5.6 %convolution_convert_fusion = bf16[128,2304]{1,0:T(8,128)(2,1)S(1)} fusion(bf16[1536,2304]{0,1:T(8,128)(2,1)} %all-gather.5.cloned.1.call-done, bf16[1,128,1536]{2,1,0:T(8,128)(2,1)} %param.18, f32[1536]{0:T(1024)S(1)} %get-tuple-element.72, f32[1536]{0:T(1024)S(1)} %get-tuple-element.76, f32[128]{0:T(128)S(1)} %add_rsqrt_fusion.3, ...), kind=kOutput, calls=%fused_computation.13 | convolution fusion | flops 907444224 | bytes 8074240 | tf_op jit(solution)/shard_map/dot_general | solution.py:92
  91.5 4.9 stack.2
  96.4 4.9 all-to-all-start
  103.1 3.3 convolution_convert_fusion.1
  109.8 1.8 copy.33
  114.6 154.5 %all-gather.7.cloned.1.call-done = bf16[2048,768]{1,0:T(8,128)(2,1)} async-done(((bf16[128,768]{1,0:T(8,128)(2,1)}), bf16[2048,768]{1,0:T(8,128)(2,1)}) %all-gather.7.cloned.1.call-update) | async-done | bytes 3145744 | tf_op jit(solution)/shard_map/all_gather | solution.py:110
  269.2 82.0 %all-gather.9.cloned.1.call-done = bf16[2048,768]{1,0:T(8,128)(2,1)} async-done(((bf16[128,768]{1,0:T(8,128)(2,1)}), bf16[2048,768]{1,0:T(8,128)(2,1)}) %all-gather.9.cloned.1.call-update) | async-done | bytes 3145744 | tf_op jit(solution)/shard_map/all_gather | solution.py:111
  351.7 138.3 %while.14 = (s32[]{:T(128)}, f32[12,128]{1,0:T(8,128)S(1)}, f32[12,128]{1,0:T(8,128)}, f32[12,128,64]{1,2,0:T(8,128)}, s32[16]{0:T(128)}, /*index=5*/s32[]{:T(12...) while((s32[]{:T(128)}, f32[12,128]{1,0:T(8,128)S(1)}, ...), condition=%wide.region_9.10_spmd, body=%wide.region_6.9_spmd.sunk | while | flops 51907840 | bytes 5407121 | solution.py:123
  358.4 2.0 convolution_add_fusion.4
  367.0 2.0 convolution_add_fusion.4
  375.6 2.0 convolution_add_fusion.4
  384.3 2.0 convolution_add_fusion.4
  392.9 2.0 convolution_add_fusion.4
  401.6 2.0 convolution_add_fusion.4
  410.3 2.0 convolution_add_fusion.4
  418.9 2.0 convolution_add_fusion.4
  427.6 2.0 convolution_add_fusion.4
  436.2 2.0 convolution_add_fusion.4
  444.9 2.0 convolution_add_fusion.4
  453.5 2.0 convolution_add_fusion.4
  462.1 2.0 convolution_add_fusion.4
  470.8 2.0 convolution_add_fusion.4
  479.4 2.0 convolution_add_fusion.4
  488.0 2.0 convolution_add_fusion.4
  491.1 1.6 fusion.76
  493.1 13.7 %fusion.77 = (f32[128]{0:T(128)S(1)}, f32[128,1536]{1,0:T(8,128)}) fusion(f32[128,1536]{1,0:T(8,128)S(1)} %get-tuple-element.127, bf16[3072,1536]{0,1:T(8,128)(2,1)} %bitcast.15, bf16[1536,3072]{0,1:T(8,128)(2,1)} %all-gather.11.cloned.1.call-done, f32[1536]{0:T(1024)S(1)} %copy-done.10, f32[1536]{0:T(1024)S(1)} %copy-done.8, f32[128]{0:T(128)S(1)} %add_rsqrt_fusion.2, ...), kind=kOutput, calls=%fused_computation.130 | convolution fusion | flops 2421030912 | bytes 20467200 | tf_op jit(solution)/shard_map/dot_general | solution.py:144
  508.3 1.5 fusion.58
  510.6 3.8 collective-permute-start
  514.4 2.0 collective-permute-start.1
  518.3 3.8 collective-permute-done.1
  523.4 2.0 concatenate.40
  (255 shorter events, 119.3 us)
Async XLA Ops:
  7.2 484.0 %copy-start = (bf16[768,1536]{1,0:T(8,128)(2,1)S(1)}, bf16[768,1536]{1,0:T(8,128)(2,1)}, u32[]{:S(2)}) copy-start(bf16[768,1536]{1,0:T(8,128)(2,1)} %param.28) | copy-start | bytes 7077892
  7.2 77.1 %all-gather.5.cloned.1.call-start = ((), (), s32[]{:S(2)}) async-start(), calls=%async_computation.1 | async-start | bytes 7520256 | tf_op jit(solution)/shard_map/all_gather | solution.py:94
  7.9 261.3 %all-gather.7.cloned.1.call-start = ((), (), s32[]{:S(2)}) async-start(), calls=%async_computation.2 | async-start | bytes 3342336 | tf_op jit(solution)/shard_map/all_gather | solution.py:110
  84.3 7.2 %copy-start.3 = (bf16[3072,96]{0,1:T(8,128)(2,1)S(1)}, bf16[3072,96]{0,1:T(8,128)(2,1)}, u32[]{:S(2)}) copy-start(bf16[3072,96]{0,1:T(8,128)(2,1)} %param.30) | copy-start | bytes 1769476
  90.8 260.5 %all-gather.9.cloned.1.call-start = ((), (), s32[]{:S(2)}) async-start(), calls=%async_computation.3 | async-start | bytes 3342336 | tf_op jit(solution)/shard_map/all_gather | solution.py:111
  96.4 6.2 %copy-start.6 = (f32[1,2,1536]{2,1,0:T(2,128)S(1)}, f32[1,2,1536]{2,1,0:T(2,128)}, u32[]{:S(2)}) copy-start(f32[1,2,1536]{2,1,0:T(2,128)} %param.22) | copy-start | bytes 36868
  96.4 6.2 %copy-start.1 = (bf16[1,154,1536]{2,1,0:T(8,128)(2,1)S(1)}, bf16[1,154,1536]{2,1,0:T(8,128)(2,1)}, u32[]{:S(2)}) copy-start(bf16[1,154,1536]{2,1,0:T(8,128)(2,1)} %param.19) | copy-start | bytes 1419268
  96.4 396.6 %all-to-all-start = ((bf16[16,3072,96]{1,2,0:T(8,128)(2,1)}), bf16[16,3072,96]{1,2,0:T(8,128)(2,1)}, u32[]{:S(2)}, u32[]{:S(2)}) async-start(bf16[16,3072,96]{1,2,0:T(8,128)(2,1)} %stack.2), calls=%async_computation | async-start | bytes 18874368 | tf_op jit(solution)/shard_map/all_to_all | solution.py:20
  101.3 391.7 %all-gather.11.cloned.1.call-start = ((), (), s32[]{:S(2)}) async-start(), calls=%async_computation.4 | async-start | bytes 10027008 | tf_op jit(solution)/shard_map/all_gather | solution.py:139
  103.1 3.8 copy-start.7
  103.1 5.7 %copy-start.4 = (f32[1,4,2048]{2,1,0:T(4,128)S(1)}, f32[1,4,2048]{2,1,0:T(4,128)}, u32[]{:S(2)}) copy-start(f32[1,4,2048]{2,1,0:T(4,128)} %param.20) | copy-start | bytes 98308
  108.2 243.5 %copy-start.13 = (pred[4]{0:T(512)(128)(4,1)}, pred[4]{0:T(512)(128)(4,1)S(1)}, u32[]{:S(2)}) copy-start(pred[4]{0:T(512)(128)(4,1)S(1)} %add_compare_fusion.1) | copy-start | bytes 16
  490.0 3.0 copy-start.8
  490.0 3.0 copy-start.9
  490.0 3.0 copy-start.10
  493.1 15.2 %copy-start.11 = (f32[1536]{0:T(1024)S(1)}, f32[1536]{0:T(1024)}, u32[]{:S(2)}) copy-start(f32[1536]{0:T(1024)} %get-tuple-element.77) | copy-start | bytes 18436
  493.1 15.2 %copy-start.12 = (f32[1536]{0:T(1024)S(1)}, f32[1536]{0:T(1024)}, u32[]{:S(2)}) copy-start(f32[1536]{0:T(1024)} %get-tuple-element.78) | copy-start | bytes 18436
  493.1 15.2 %copy-start.16 = (bf16[1536,64]{0,1:T(8,128)(2,1)S(1)}, bf16[1536,64]{0,1:T(8,128)(2,1)}, u32[]{:S(2)}) copy-start(bf16[1536,64]{0,1:T(8,128)(2,1)} %param.31) | copy-start | bytes 589828
  493.1 17.4 %copy-start.5 = (f32[1,4,2048]{2,1,0:T(4,128)S(1)}, f32[1,4,2048]{2,1,0:T(4,128)}, u32[]{:S(2)}) copy-start(f32[1,4,2048]{2,1,0:T(4,128)} %param.20) | copy-start | bytes 98308
  493.1 17.4 %copy-start.14 = (pred[4]{0:T(512)(128)(4,1)S(1)}, pred[4]{0:T(512)(128)(4,1)}, u32[]{:S(2)}) copy-start(pred[4]{0:T(512)(128)(4,1)} %copy-done.13) | copy-start | bytes 16
  506.8 10.7 %copy-start.2 = (f32[512,16]{1,0:T(8,128)S(1)}, f32[512,16]{1,0:T(8,128)}, u32[]{:S(2)}) copy-start(f32[512,16]{1,0:T(8,128)} %squeeze.13) | copy-start | bytes 98308
  506.8 10.7 %copy-start.15 = (pred[512]{0:T(512)(128)(4,1)S(1)}, pred[512]{0:T(512)(128)(4,1)}, u32[]{:S(2)}) copy-start(pred[512]{0:T(512)(128)(4,1)} %broadcast_bitcast_fusion) | copy-start | bytes 1540
  508.3 17.2 %copy-start.17 = (f32[512]{0:T(512)S(1)}, f32[512]{0:T(512)}, u32[]{:S(2)}) copy-start(f32[512]{0:T(512)} %param.33) | copy-start | bytes 6148
  510.6 7.7 %collective-permute-start = (bf16[1,2048]{1,0:T(2,128)(2,1)S(1)}, bf16[1,2048]{1,0:T(2,128)(2,1)S(1)}, u32[]{:S(2)}, u32[]{:S(2)}) collective-permute-start(bf16[1,2048]{1,0:T(2,128)(2,1)S(1)} %get-tuple-element.120), channel_id=1, source_target_pairs={{0,16},{16,32},{32,48},{48,64},{64,80},{80,96},{96,112},{112,128},... | collective-permute-start | bytes 12296 | tf_op jit(solution)/shard_map/ppermute | solution.py:30
  514.4 7.7 %collective-permute-start.1 = (bf16[1,2048]{1,0:T(2,128)(2,1)S(1)}, bf16[1,2048]{1,0:T(2,128)(2,1)S(1)}, u32[]{:S(2)}, u32[]{:S(2)}) collective-permute-start(bf16[1,2048]{1,0:T(2,128)(2,1)S(1)} %get-tuple-element.121), channel_id=1, source_target_pairs={{16,0},{32,16},{48,32},{64,48},{80,64},{96,80},{112,96},{128,112},... | collective-permute-start | bytes 12296 | tf_op jit(solution)/shard_map/ppermute | solution.py:31
Sparse Core Ops, SparseCore 0:
  10.7 73.5 all-gather.4
  90.9 178.2 all-gather.6
  271.0 80.2 all-gather.8
  353.8 81.4 all-gather.10
